TPU v7x, 32 devices: a whole 2x2x4 slice. The times are simulated.
32 devices in a mesh: dp: 8 (over z, x), fsdp: 4 (over y, core).
Axes of the slice: x: 2, y: 2, z: 4, core: 2. Of those that a mesh axis runs over, the one named last changes fastest.
Arguments:
- acts: bfloat16 [1024, 3072], P('dp'), may hold values from -6 to 6
- weight: bfloat16 [3072, 3072], P('dp', 'fsdp'), may hold values from -0.15625 to 0.15625
- block_mask: int32 [4, 12, 12], replicated, may hold values 0 or 1
- out_grad: bfloat16 [4, 1024, 3072], P(None, 'dp', 'fsdp'), may hold values from -6 to 6
Outputs:
- outputs: bfloat16 [4, 1024, 3072], P(None, 'dp', 'fsdp')
- grad_w: float32 [3072, 3072], P('dp', 'fsdp')
- grad_x: bfloat16 [1024, 3072], P('dp', 'fsdp')
All inputs are finite; a program needn't handle non-finite values.
Results may differ from a plain program's by a relative error of at most 0.001.
Values may be sent and summed in bfloat16 or wider, within the bound.
No kernel may reach another device: no remote copies, remote signals or barrier semaphores. Data moves between devices by JAX's collectives and lax.ppermute only.
A program may use at most 128 MiB of HBM per device.

v0:
```python
import jax
import jax.numpy as jnp
from jax import lax
from jax.sharding import PartitionSpec as P

BS = 256
TOK_G = 128


def on_device(acts, weight, block_mask, out_grad):
    width = weight.shape[1]
    kblocks = block_mask.shape[1]
    oblocks = block_mask.shape[2]
    first_col = lax.axis_index("fsdp") * width
    col_ids = (first_col + jnp.arange(width, dtype=jnp.int32)) // BS
    col_select = (col_ids[None, :] == jnp.arange(oblocks, dtype=jnp.int32)[:, None]).astype(
        jnp.float32
    )
    col_mask = jnp.einsum("skb,bc->skc", block_mask.astype(jnp.float32), col_select)

    def piece_mask(count):
        row_ids = jnp.arange(count, dtype=jnp.int32) // BS
        row_select = (row_ids[:, None] == jnp.arange(kblocks, dtype=jnp.int32)[None, :]).astype(
            jnp.float32
        )
        return jnp.einsum("nk,skc->snc", row_select, col_mask)

    def masked_piece(piece):
        return piece_mask(piece.shape[0]).astype(jnp.bfloat16) * piece[None]

    cols = acts
    forward = jnp.einsum(
        "tn,snc->stc",
        cols,
        masked_piece(lax.all_gather(weight, "dp", axis=0, tiled=True)),
        preferred_element_type=jnp.float32,
    )
    input_part = jnp.einsum(
        "stc,snc->tn",
        out_grad,
        masked_piece(lax.all_gather(weight, "dp", axis=0, tiled=True)),
        preferred_element_type=jnp.float32,
    )
    outputs = forward.astype(jnp.bfloat16)
    cols = acts
    products = jnp.einsum("tn,stc->snc", cols, out_grad, preferred_element_type=jnp.float32)
    grad_w = lax.psum_scatter(
        jnp.sum(piece_mask(lax.axis_size("dp") * weight.shape[0]) * products, axis=0)
        * (1.0 / TOK_G),
        "dp",
        scatter_dimension=0,
        tiled=True,
    )
    grad_x = lax.psum_scatter(input_part, "fsdp", scatter_dimension=1, tiled=True).astype(
        jnp.bfloat16
    )
    return (outputs, grad_w, grad_x)


def solution(mesh):
    in_specs = (P("dp", None), P("dp", "fsdp"), P(), P(None, "dp", "fsdp"))
    out_specs = (P(None, "dp", "fsdp"), P("dp", "fsdp"), P("dp", "fsdp"))
    return jax.shard_map(
        on_device, mesh=mesh, in_specs=in_specs, out_specs=out_specs, check_vma=False
    )
```

profile of v0, /device:TPU:0, one launch (start us, length us, event | category | flops | bytes accessed | tf_op | source)
XLA Modules:
  0.0 319.4 jit_solution(12060055116255987593)
XLA Ops:
  7.2 0.0 copy-start
  7.2 0.0 all-gather.2.cloned.1.call-start
  7.2 0.7 all-gather.2.cloned.1.call-update
  7.9 0.0 reduce-scatter.5.cloned.1.call-start
  8.0 0.7 convert_element_type.23
  8.7 15.5 %fusion.5 = f32[4,768,3072]{2,1,0:T(8,128)} fusion(s32[3072]{0:T(1024)S(1)} %add_select_fusion, bf16[4,12,12]{2,0,1:T(4,128)(2,1)S(1)} %convert_element_type.23, s32[768]{0:T(1024)S(1)} %add_select_fusion.1), kind=kOutput, calls=%fused_computation.9 | convolution fusion | flops 227423232 | bytes 37765248 | tf_op jit(solution)/shard_map/nk,skc->snc/dot_general | solution.py:26
  24.2 68.6 %all-gather.2.cloned.1.call-done = bf16[3072,768]{1,0:T(8,128)(2,1)} async-done(((bf16[384,768]{1,0:T(8,128)(2,1)}), bf16[3072,768]{1,0:T(8,128)(2,1)}) %all-gather.2.cloned.1.call-update) | async-done | bytes 4718608 | tf_op jit(solution)/shard_map/all_gather | solution.py:35
  92.8 6.6 %copy.12 = bf16[3072,768]{0,1:T(8,128)(2,1)} copy(bf16[3072,768]{1,0:T(8,128)(2,1)} %all-gather.2.cloned.1.call-done) | data formatting | bytes 9437184 | tf_op jit(solution)/shard_map/all_gather | solution.py:35
  99.5 0.0 copy-done
  99.5 0.0 copy-start.1
  99.5 16.7 %fusion.2 = f32[128,3072]{0,1:T(8,128)} fusion(bf16[4,128,768]{2,1,0:T(8,128)(2,1)S(1)} %copy-done, f32[4,768,3072]{2,1,0:T(8,128)} %fusion.5, bf16[3072,768]{0,1:T(8,128)(2,1)} %copy.12), kind=kOutput, calls=%fused_computation.5 | convolution fusion | flops 2434793472 | bytes 44826624 | tf_op jit(solution)/shard_map/stc,snc->tn/dot_general | solution.py:38
  116.2 0.0 reduce-scatter.5.cloned.1.call-update
  116.2 0.0 reduce-scatter.3.cloned.1.call-start
  116.3 0.0 copy-done.1
  116.3 18.9 %multiply_reduce_fusion = f32[768,3072]{1,0:T(8,128)} fusion(f32[4,768,3072]{2,1,0:T(8,128)} %fusion.5, bf16[4,128,768]{2,1,0:T(8,128)(2,1)S(1)} %copy-done, bf16[128,3072]{1,0:T(8,128)(2,1)S(1)} %copy-done.1), kind=kOutput, calls=%fused_computation | convolution fusion | flops 2432434176 | bytes 48758784 | tf_op jit(solution)/shard_map/tn,stc->snc/dot_general | solution.py:46
  135.2 9.0 %multiply_bitcast_fusion = f32[3072,768]{0,1:T(8,128)} fusion(f32[768,3072]{1,0:T(8,128)} %multiply_reduce_fusion), kind=kLoop, calls=%fused_computation.2 | loop fusion | flops 2359296 | bytes 18874368 | tf_op jit(solution)/shard_map/mul | solution.py:48
  144.2 0.0 reduce-scatter.3.cloned.1.call-update
  144.2 16.1 %fusion.4 = bf16[4,128,768]{1,2,0:T(8,128)(2,1)S(1)} fusion(f32[4,768,3072]{2,1,0:T(8,128)} %fusion.5, bf16[3072,768]{0,1:T(8,128)(2,1)} %copy.12, bf16[128,3072]{1,0:T(8,128)(2,1)S(1)} %copy-done.1), kind=kOutput, calls=%fused_computation.7 | convolution fusion | flops 2435186688 | bytes 44040192 | tf_op jit(solution)/shard_map/tn,snc->stc/dot_general | solution.py:32
  160.3 1.2 copy.15
  161.4 0.0 reduce-scatter.5.cloned.1.call-done
  161.4 1.0 convert_element_type.28
  162.5 0.8 copy.17
  163.3 146.9 %reduce-scatter.3.cloned.1.call-done = f32[384,768]{0,1:T(8,128)} async-done(((f32[3072,768]{0,1:T(8,128)}), f32[384,768]{0,1:T(8,128)}) %reduce-scatter.3.cloned.1.call-update) | async-done | bytes 1179664 | tf_op jit(solution)/shard_map/reduce_scatter | solution.py:47
  310.2 2.7 copy.16
  (2 shorter events, 0.0 us)
Async XLA Ops:
  7.2 92.3 %copy-start = (bf16[4,128,768]{2,1,0:T(8,128)(2,1)S(1)}, bf16[4,128,768]{2,1,0:T(8,128)(2,1)}, u32[]{:S(2)}) copy-start(bf16[4,128,768]{2,1,0:T(8,128)(2,1)} %param.7) | copy-start | bytes 2359300
  7.2 85.6 %all-gather.2.cloned.1.call-start = ((), (), s32[]{:S(2)}) async-start(), calls=%async_computation.2 | async-start | bytes 5308416 | tf_op jit(solution)/shard_map/all_gather | solution.py:35
  7.9 153.5 %reduce-scatter.5.cloned.1.call-start = ((), (), s32[]{:S(2)}) async-start(), calls=%async_computation.4 | async-start | bytes 1966080 | tf_op jit(solution)/shard_map/reduce_scatter | solution.py:54
  99.5 16.8 %copy-start.1 = (bf16[128,3072]{1,0:T(8,128)(2,1)S(1)}, bf16[128,3072]{1,0:T(8,128)(2,1)}, u32[]{:S(2)}) copy-start(bf16[128,3072]{1,0:T(8,128)(2,1)} %param.4) | copy-start | bytes 2359300
  116.2 194.0 %reduce-scatter.3.cloned.1.call-start = ((), (), s32[]{:S(2)}) async-start(), calls=%async_computation.3 | async-start | bytes 10616832 | tf_op jit(solution)/shard_map/reduce_scatter | solution.py:47
Sparse Core Ops, SparseCore 0:
  10.2 82.5 all-gather.1
  116.3 26.2 reduce-scatter.4
  146.7 163.4 reduce-scatter.2
where the time goes:
time: 320 us; the launch traced here: 319 us
  waiting for transfers between devices  216 us (68%)
  matrix products  67.2 us (21%)
  between operations  13.8 us (4%)
  local copies, waits for them, and re-layouts  11.3 us (4%)
  other arithmetic  10.8 us (3%)
    reduce_scatter x1, waiting for transfers between devices, on_device(): lax.psum_scatter(jnp.sum(piece_mask(lax.axis_size('dp') * weight.shape[0]...  147 us
    all_gather x1, waiting for transfers between devices, on_device(): lax.all_gather(weight, 'dp', axis=0, tiled=True)  68.6 us
    dot_general x1, matrix products, on_device(): jnp.einsum('tn,stc->snc', cols, out_grad, preferred_element_type=jnp.floa...  18.9 us
    dot_general x1, matrix products, on_device(): jnp.einsum('stc,snc->tn', out_grad, masked_piece(lax.all_gather(weight, '...  16.7 us
    dot_general x1, matrix products, on_device(): jnp.einsum('tn,snc->stc', cols, masked_piece(lax.all_gather(weight, 'dp',...  16.1 us
    dot_general x1, matrix products, piece_mask(): return jnp.einsum('nk,skc->snc', row_select, col_mask)  15.5 us
    mul x1, other arithmetic, on_device(): jnp.sum(piece_mask(lax.axis_size('dp') * weight.shape[0]) * products, axi...  8.99 us
    all_gather x1, local copies, waits for them, and re-layouts, on_device(): lax.all_gather(weight, 'dp', axis=0, tiled=True)  6.65 us
  transfers between devices with their start and end apart: 3, of which 2 were waited for; matrix products, arithmetic and copies ran while one was open for 20% of the time, Pallas kernels for 0%

commit v1 on v0

--- a/solution.py
+++ b/solution.py
@@ -5,6 +5,27 @@
 
 BS = 256
 TOK_G = 128
+
+
+def collect(x, axis, dim):
+    peers, position, span = (lax.axis_size(axis), lax.axis_index(axis), x.shape[dim])
+    right = [(i, (i + 1) % peers) for i in range(peers)]
+    backward = [(i, (i - 1) % peers) for i in range(peers)]
+    out = jnp.zeros((*x.shape[:dim], peers * span, *x.shape[dim + 1 :]), x.dtype)
+    out = lax.dynamic_update_slice_in_dim(out, x, position * span, axis=dim)
+    from_left = from_right = x
+    half = peers // 2
+    for hop in range(1, half + 1):
+        from_left = lax.ppermute(from_left, axis, right)
+        out = lax.dynamic_update_slice_in_dim(
+            out, from_left, (position - hop) % peers * span, axis=dim
+        )
+        if hop < peers - half:
+            from_right = lax.ppermute(from_right, axis, backward)
+            out = lax.dynamic_update_slice_in_dim(
+                out, from_right, (position + hop) % peers * span, axis=dim
+            )
+    return out
 
 
 def on_device(acts, weight, block_mask, out_grad):
@@ -32,7 +53,7 @@
     forward = jnp.einsum(
         "tn,snc->stc",
         cols,
-        masked_piece(lax.all_gather(weight, "dp", axis=0, tiled=True)),
+        masked_piece(collect(weight, "dp", 0)),
         preferred_element_type=jnp.float32,
     )
     input_part = jnp.einsum(

time: 320 us -> 368 us (1.15)
  local copies, waits for them, and re-layouts: 11.3 us -> 29.3 us
  waiting for transfers between devices: 216 us -> 233 us
  starting transfers between devices: 0.12 us -> 13.3 us
    ppermute x0 -> x7, waiting for transfers between devices: none -> 101 us  [the longest x4 86 us: collect(): from_left = lax.ppermute(from_left, axis, right)]
    reduce_scatter x1, waiting for transfers between devices: 147 us -> 63 us  [on_device(): lax.psum_scatter(jnp.sum(piece_mask(lax.axis_size('dp') * weight.shape[0]...]
    ppermute x0 -> x7, starting transfers between devices: none -> 13.1 us  [the longest x3 10.1 us: collect(): from_right = lax.ppermute(from_right, axis, backward)]
    dynamic_update_slice x0 -> x8, local copies, waits for them, and re-layouts: none -> 7.59 us  [the longest x4 3.76 us: collect(): lax.dynamic_update_slice_in_dim(out, from_left, (position - hop) % peers...]
    ppermute x0 -> x7, local copies, waits for them, and re-layouts: none -> 6.39 us  [the longest x4 3.34 us: collect(): from_left = lax.ppermute(from_left, axis, right)]
  transfers between devices with their start and end apart: 3 -> 10, of which waited for: 2 -> 9; matrix products, arithmetic and copies ran while one was open for 20% -> 22% of each run, Pallas kernels for 0% -> 0%
where the time goes in v1:
time: 368 us
  waiting for transfers between devices  233 us (63%)
  matrix products  67.2 us (18%)
  local copies, waits for them, and re-layouts  29.3 us (8%)
  between operations  14 us (4%)
  starting transfers between devices  13.3 us (4%)
  other arithmetic  10.8 us (3%)
    ppermute x4, waiting for transfers between devices, collect(): from_left = lax.ppermute(from_left, axis, right)  86 us
    all_gather x1, waiting for transfers between devices, on_device(): lax.all_gather(weight, 'dp', axis=0, tiled=True)  68.6 us
    reduce_scatter x1, waiting for transfers between devices, on_device(): lax.psum_scatter(jnp.sum(piece_mask(lax.axis_size('dp') * weight.shape[0]...  63 us
    dot_general x1, matrix products, on_device(): jnp.einsum('tn,stc->snc', cols, out_grad, preferred_element_type=jnp.floa...  18.9 us
    dot_general x1, matrix products, on_device(): jnp.einsum('stc,snc->tn', out_grad, masked_piece(lax.all_gather(weight, '...  16.8 us
    dot_general x1, matrix products, on_device(): jnp.einsum('tn,snc->stc', cols, masked_piece(collect(weight, 'dp', 0)), p...  16 us
    dot_general x1, matrix products, piece_mask(): return jnp.einsum('nk,skc->snc', row_select, col_mask)  15.5 us
    ppermute x3, waiting for transfers between devices, collect(): from_right = lax.ppermute(from_right, axis, backward)  15 us
  transfers between devices with their start and end apart: 10, of which 9 were waited for; matrix products, arithmetic and copies ran while one was open for 22% of the time, Pallas kernels for 0%

profile of v1, /device:TPU:0, one launch (start us, length us, event | category | flops | bytes accessed | tf_op | source)
XLA Modules:
  0.0 367.8 jit_solution(496707984934986260)
XLA Ops:
  7.2 0.0 copy-start
  7.2 0.0 all-gather.2.cloned.1.call-start
  7.2 0.7 all-gather.2.cloned.1.call-update
  7.9 0.0 reduce-scatter.5.cloned.1.call-start
  8.0 0.7 convert_element_type.23
  8.7 15.5 %fusion.9 = f32[4,768,3072]{2,1,0:T(8,128)} fusion(s32[3072]{0:T(1024)S(1)} %add_select_fusion, bf16[4,12,12]{2,0,1:T(4,128)(2,1)S(1)} %convert_element_type.23, s32[768]{0:T(1024)S(1)} %add_select_fusion.1), kind=kOutput, calls=%fused_computation.14 | convolution fusion | flops 227423232 | bytes 37765248 | tf_op jit(solution)/shard_map/nk,skc->snc/dot_general | solution.py:47
  24.2 68.6 %all-gather.2.cloned.1.call-done = bf16[3072,768]{1,0:T(8,128)(2,1)} async-done(((bf16[384,768]{1,0:T(8,128)(2,1)}), bf16[3072,768]{1,0:T(8,128)(2,1)}) %all-gather.2.cloned.1.call-update) | async-done | bytes 4718608 | tf_op jit(solution)/shard_map/all_gather | solution.py:62
  92.8 6.7 %copy.29 = bf16[3072,768]{0,1:T(8,128)(2,1)} copy(bf16[3072,768]{1,0:T(8,128)(2,1)} %all-gather.2.cloned.1.call-done) | data formatting | bytes 9437184 | tf_op jit(solution)/shard_map/all_gather | solution.py:62
  99.5 0.0 copy-done
  99.5 0.0 copy-start.2
  99.5 16.8 %fusion.6 = f32[128,3072]{0,1:T(8,128)} fusion(bf16[4,128,768]{2,1,0:T(8,128)(2,1)S(1)} %copy-done, bf16[3072,768]{0,1:T(8,128)(2,1)} %copy.29, f32[4,768,3072]{2,1,0:T(8,128)} %fusion.9), kind=kOutput, calls=%fused_computation.10 | convolution fusion | flops 2434793472 | bytes 44826624 | tf_op jit(solution)/shard_map/stc,snc->tn/dot_general | solution.py:59
  116.3 0.0 reduce-scatter.5.cloned.1.call-update
  116.3 0.0 reduce-scatter.3.cloned.1.call-start
  116.3 0.0 copy-done.2
  116.3 18.9 %multiply_reduce_fusion = f32[768,3072]{1,0:T(8,128)} fusion(f32[4,768,3072]{2,1,0:T(8,128)} %fusion.9, bf16[4,128,768]{2,1,0:T(8,128)(2,1)S(1)} %copy-done, bf16[128,3072]{1,0:T(8,128)(2,1)S(1)} %copy-done.2), kind=kOutput, calls=%fused_computation | convolution fusion | flops 2432434176 | bytes 48758784 | tf_op jit(solution)/shard_map/tn,stc->snc/dot_general | solution.py:67
  135.3 9.0 %multiply_bitcast_fusion = f32[3072,768]{0,1:T(8,128)} fusion(f32[768,3072]{1,0:T(8,128)} %multiply_reduce_fusion), kind=kLoop, calls=%fused_computation.6 | loop fusion | flops 2359296 | bytes 18874368 | tf_op jit(solution)/shard_map/mul | solution.py:69
  144.3 0.0 copy-start.3
  144.3 0.0 reduce-scatter.3.cloned.1.call-update
  144.3 1.0 copy-done.3
  145.4 0.6 collective-permute-start
  145.9 4.2 %collective-permute-start.1 = (bf16[384,768]{1,0:T(8,128)(2,1)S(1)}, bf16[384,768]{1,0:T(8,128)(2,1)}, u32[]{:S(2)}, u32[]{:S(2)}) collective-permute-start(bf16[384,768]{1,0:T(8,128)(2,1)S(1)} %copy-done.3), channel_id=1, source_target_pairs={{0,28},{4,0},{8,4},{12,8},{16,12},{20,16},{24,20},{28,24},{1,29},{... | collective-permute-start | bytes 1769480 | tf_op jit(solution)/shard_map/ppermute | solution.py:24
  150.1 33.9 %collective-permute-done = bf16[384,768]{1,0:T(8,128)(2,1)S(1)} collective-permute-done((bf16[384,768]{1,0:T(8,128)(2,1)S(1)}, bf16[384,768]{1,0:T(8,128)(2,1)S(1)}, u32[]{:S(2)}, u32[]{:S(2)}) %collective-permute-start) | collective-permute-done | bytes 589856 | tf_op jit(solution)/shard_map/ppermute | solution.py:19
  184.0 0.0 copy-start.4
  184.0 2.5 collective-permute-start.2
  186.5 2.8 collective-permute-done.1
  189.3 2.9 collective-permute-start.3
  192.2 0.0 copy-done.4
  192.2 21.1 %collective-permute-done.2 = bf16[384,768]{1,0:T(8,128)(2,1)} collective-permute-done((bf16[384,768]{1,0:T(8,128)(2,1)S(1)}, bf16[384,768]{1,0:T(8,128)(2,1)}, u32[]{:S(2)}, u32[]{:S(2)}) %collective-permute-start.2) | collective-permute-done | bytes 589856 | tf_op jit(solution)/shard_map/ppermute | solution.py:19
  213.3 0.0 collective-permute-start.4
  213.4 0.3 copy.20
  213.7 0.0 copy-start.5
  213.8 6.6 %collective-permute-done.3 = bf16[384,768]{1,0:T(8,128)(2,1)S(1)} collective-permute-done((bf16[384,768]{1,0:T(8,128)(2,1)}, bf16[384,768]{1,0:T(8,128)(2,1)S(1)}, u32[]{:S(2)}, u32[]{:S(2)}) %collective-permute-start.3) | collective-permute-done | bytes 589856 | tf_op jit(solution)/shard_map/ppermute | solution.py:24
  220.4 3.0 collective-permute-start.5
  223.4 2.7 mul.59
  226.1 0.9 constant_dynamic-update-slice_fusion.7
  227.0 0.0 copy-done.5
  227.0 0.3 copy.21
  227.3 1.4 copy.22
  228.7 0.9 constant_dynamic-update-slice_fusion.6
  229.6 13.7 %collective-permute-done.4 = bf16[384,768]{1,0:T(8,128)(2,1)S(1)} collective-permute-done((bf16[384,768]{1,0:T(8,128)(2,1)}, bf16[384,768]{1,0:T(8,128)(2,1)S(1)}, u32[]{:S(2)}, u32[]{:S(2)}) %collective-permute-start.4) | collective-permute-done | bytes 589856 | tf_op jit(solution)/shard_map/ppermute | solution.py:19
  243.3 0.0 collective-permute-start.6
  243.3 1.1 constant_dynamic-update-slice_fusion.5
  244.4 1.4 copy.23
  245.7 0.3 copy.24
  246.0 0.9 constant_dynamic-update-slice_fusion.4
  247.0 0.9 constant_dynamic-update-slice_fusion.3
  247.9 0.3 copy.25
  248.2 5.7 %collective-permute-done.5 = bf16[384,768]{1,0:T(8,128)(2,1)} collective-permute-done((bf16[384,768]{1,0:T(8,128)(2,1)S(1)}, bf16[384,768]{1,0:T(8,128)(2,1)}, u32[]{:S(2)}, u32[]{:S(2)}) %collective-permute-start.5) | collective-permute-done | bytes 589856 | tf_op jit(solution)/shard_map/ppermute | solution.py:24
  253.9 1.4 copy.26
  255.2 0.9 constant_dynamic-update-slice_fusion.2
  256.2 0.9 constant_dynamic-update-slice_fusion.1
  257.1 17.2 %collective-permute-done.6 = bf16[384,768]{1,0:T(8,128)(2,1)} collective-permute-done((bf16[384,768]{1,0:T(8,128)(2,1)S(1)}, bf16[384,768]{1,0:T(8,128)(2,1)}, u32[]{:S(2)}, u32[]{:S(2)}) %collective-permute-start.6) | collective-permute-done | bytes 589856 | tf_op jit(solution)/shard_map/ppermute | solution.py:19
  274.3 1.4 copy.27
  275.7 1.0 constant_dynamic-update-slice_fusion
  276.6 0.0 copy-start.1
  276.7 16.0 %fusion.8 = bf16[4,128,768]{1,2,0:T(8,128)(2,1)S(1)} fusion(bf16[3072,768]{0,1:T(8,128)(2,1)} %constant_dynamic-update-slice_fusion, f32[4,768,3072]{2,1,0:T(8,128)} %fusion.9, bf16[128,3072]{1,0:T(8,128)(2,1)S(1)} %copy-done.2), kind=kOutput, calls=%fused_computation.12 | convolution fusion | flops 2435186688 | bytes 44040192 | tf_op jit(solution)/shard_map/tn,snc->stc/dot_general | solution.py:53
  292.6 1.2 copy.31
  293.8 0.0 reduce-scatter.5.cloned.1.call-done
  293.8 1.0 convert_element_type.28
  294.8 0.8 copy.33
  295.6 63.0 %reduce-scatter.3.cloned.1.call-done = f32[384,768]{0,1:T(8,128)} async-done(((f32[3072,768]{0,1:T(8,128)}), f32[384,768]{0,1:T(8,128)}) %reduce-scatter.3.cloned.1.call-update) | async-done | bytes 1179664 | tf_op jit(solution)/shard_map/reduce_scatter | solution.py:68
  358.6 2.7 copy.32
  361.3 0.0 copy-done.1
  (2 shorter events, 0.0 us)
Async XLA Ops:
  7.2 92.3 %copy-start = (bf16[4,128,768]{2,1,0:T(8,128)(2,1)S(1)}, bf16[4,128,768]{2,1,0:T(8,128)(2,1)}, u32[]{:S(2)}) copy-start(bf16[4,128,768]{2,1,0:T(8,128)(2,1)} %param.7) | copy-start | bytes 2359300
  7.2 85.6 %all-gather.2.cloned.1.call-start = ((), (), s32[]{:S(2)}) async-start(), calls=%async_computation.3 | async-start | bytes 5308416 | tf_op jit(solution)/shard_map/all_gather | solution.py:62
  7.9 285.9 %reduce-scatter.5.cloned.1.call-start = ((), (), s32[]{:S(2)}) async-start(), calls=%async_computation.4 | async-start | bytes 1966080 | tf_op jit(solution)/shard_map/reduce_scatter | solution.py:75
  99.5 16.9 %copy-start.2 = (bf16[128,3072]{1,0:T(8,128)(2,1)S(1)}, bf16[128,3072]{1,0:T(8,128)(2,1)}, u32[]{:S(2)}) copy-start(bf16[128,3072]{1,0:T(8,128)(2,1)} %param.4) | copy-start | bytes 2359300
  116.3 242.3 %reduce-scatter.3.cloned.1.call-start = ((), (), s32[]{:S(2)}) async-start(), calls=%async_computation.2 | async-start | bytes 10616832 | tf_op jit(solution)/shard_map/reduce_scatter | solution.py:68
  144.3 1.1 copy-start.3
  145.4 38.7 %collective-permute-start = (bf16[384,768]{1,0:T(8,128)(2,1)S(1)}, bf16[384,768]{1,0:T(8,128)(2,1)S(1)}, u32[]{:S(2)}, u32[]{:S(2)}) collective-permute-start(bf16[384,768]{1,0:T(8,128)(2,1)S(1)} %copy-done.3), channel_id=1, source_target_pairs={{0,4},{4,8},{8,12},{12,16},{16,20},{20,24},{24,28},{28,0},{1,5},{5... | collective-permute-start | bytes 1769480 | tf_op jit(solution)/shard_map/ppermute | solution.py:19
  145.9 43.4 %collective-permute-start.1 = (bf16[384,768]{1,0:T(8,128)(2,1)S(1)}, bf16[384,768]{1,0:T(8,128)(2,1)}, u32[]{:S(2)}, u32[]{:S(2)}) collective-permute-start(bf16[384,768]{1,0:T(8,128)(2,1)S(1)} %copy-done.3), channel_id=1, source_target_pairs={{0,28},{4,0},{8,4},{12,8},{16,12},{20,16},{24,20},{28,24},{1,29},{... | collective-permute-start | bytes 1769480 | tf_op jit(solution)/shard_map/ppermute | solution.py:24
  184.0 8.2 %copy-start.4 = (bf16[384,768]{1,0:T(8,128)(2,1)}, bf16[384,768]{1,0:T(8,128)(2,1)S(1)}, u32[]{:S(2)}) copy-start(bf16[384,768]{1,0:T(8,128)(2,1)S(1)} %collective-permute-done) | copy-start | bytes 1769476
  184.0 29.3 %collective-permute-start.2 = (bf16[384,768]{1,0:T(8,128)(2,1)S(1)}, bf16[384,768]{1,0:T(8,128)(2,1)}, u32[]{:S(2)}, u32[]{:S(2)}) collective-permute-start(bf16[384,768]{1,0:T(8,128)(2,1)S(1)} %collective-permute-done), channel_id=1, source_target_pairs={{0,4},{4,8},{8,12},{12,16},{16,20},{20,24},{24,28},{28,0},{1,5},{5... | collective-permute-start | bytes 1769480 | tf_op jit(solution)/shard_map/ppermute | solution.py:19
  189.3 31.1 %collective-permute-start.3 = (bf16[384,768]{1,0:T(8,128)(2,1)}, bf16[384,768]{1,0:T(8,128)(2,1)S(1)}, u32[]{:S(2)}, u32[]{:S(2)}) collective-permute-start(bf16[384,768]{1,0:T(8,128)(2,1)} %collective-permute-done.1), channel_id=1, source_target_pairs={{0,28},{4,0},{8,4},{12,8},{16,12},{20,16},{24,20},{28,24},{1,29},{... | collective-permute-start | bytes 1769480 | tf_op jit(solution)/shard_map/ppermute | solution.py:24
  213.3 29.9 %collective-permute-start.4 = (bf16[384,768]{1,0:T(8,128)(2,1)}, bf16[384,768]{1,0:T(8,128)(2,1)S(1)}, u32[]{:S(2)}, u32[]{:S(2)}) collective-permute-start(bf16[384,768]{1,0:T(8,128)(2,1)} %collective-permute-done.2), channel_id=1, source_target_pairs={{0,4},{4,8},{8,12},{12,16},{16,20},{20,24},{24,28},{28,0},{1,5},{5... | collective-permute-start | bytes 1769480 | tf_op jit(solution)/shard_map/ppermute | solution.py:19
  213.7 13.3 %copy-start.5 = (bf16[384,768]{1,0:T(8,128)(2,1)S(1)}, bf16[384,768]{1,0:T(8,128)(2,1)}, u32[]{:S(2)}) copy-start(bf16[384,768]{1,0:T(8,128)(2,1)} %copy-done.4) | copy-start | bytes 1769476
  220.4 33.5 %collective-permute-start.5 = (bf16[384,768]{1,0:T(8,128)(2,1)S(1)}, bf16[384,768]{1,0:T(8,128)(2,1)}, u32[]{:S(2)}, u32[]{:S(2)}) collective-permute-start(bf16[384,768]{1,0:T(8,128)(2,1)S(1)} %collective-permute-done.3), channel_id=1, source_target_pairs={{0,28},{4,0},{8,4},{12,8},{16,12},{20,16},{24,20},{28,24},{1,29},{... | collective-permute-start | bytes 1769480 | tf_op jit(solution)/shard_map/ppermute | solution.py:24
  243.3 31.0 %collective-permute-start.6 = (bf16[384,768]{1,0:T(8,128)(2,1)S(1)}, bf16[384,768]{1,0:T(8,128)(2,1)}, u32[]{:S(2)}, u32[]{:S(2)}) collective-permute-start(bf16[384,768]{1,0:T(8,128)(2,1)S(1)} %collective-permute-done.4), channel_id=1, source_target_pairs={{0,4},{4,8},{8,12},{12,16},{16,20},{20,24},{24,28},{28,0},{1,5},{5... | collective-permute-start | bytes 1769480 | tf_op jit(solution)/shard_map/ppermute | solution.py:19
  276.6 84.6 %copy-start.1 = (bf16[4,128,768]{2,1,0:T(8,128)(2,1)S(1)}, bf16[4,128,768]{2,1,0:T(8,128)(2,1)}, u32[]{:S(2)}) copy-start(bf16[4,128,768]{2,1,0:T(8,128)(2,1)} %param.7) | copy-start | bytes 2359300
Sparse Core Ops, SparseCore 0:
  10.2 82.5 all-gather.1
  116.4 26.2 reduce-scatter.4
  146.8 211.8 reduce-scatter.2
